TPU v7x, 256 devices: a whole 4x4x8 slice. The times are simulated.
256 devices in a mesh: grp: 4 (over x), ep: 64 (over y, z, core).
Axes of the slice: x: 4, y: 4, z: 8, core: 2. Of those that a mesh axis runs over, the one named last changes fastest.
Arguments:
- queries: bfloat16 [6144, 4096], P(('grp', 'ep')), may hold values from -9 to 9
- new_keys: bfloat16 [6144, 512], P(('grp', 'ep')), may hold values from -9 to 9
- new_values: bfloat16 [6144, 512], P(('grp', 'ep')), may hold values from -6 to 6
- key_cache: bfloat16 [4096, 48, 512], P(('grp', 'ep')), may hold values from -9 to 9
- value_cache: bfloat16 [4096, 48, 512], P(('grp', 'ep')), may hold values from -6 to 6
- cache_len: int32 [4096], P(('grp', 'ep')), may hold values from 2 to 48, as said below
- residual: bfloat16 [6144, 2048], P(('grp', 'ep')), may hold values from -17 to 17
- out_proj: bfloat16 [4096, 2048], P(None, 'grp'), may hold values from -0.09375 to 0.09375
- norm_gain: float32 [2048], P('grp'), may hold values from 0.1 to 1.9
- expert_ids: int32 [6144, 8], P(('grp', 'ep')), may hold values from 0 to 127, as said below
- route_weights: bfloat16 [6144, 8], P(('grp', 'ep')), may hold values from 0.049804688 to 1
- slot_expert: int32 [192], replicated, may hold values from 0 to 127, as said below
- gate_up: bfloat16 [192, 2048, 1536], P('ep', 'grp'), may hold values from -1 to 1, as said below
- down_proj: bfloat16 [192, 768, 2048], P('ep', None, 'grp'), may hold values from -2 to 2, as said below
Outputs:
- moe_out: bfloat16 [6144, 2048], P(('grp', 'ep'))
- layer_out: bfloat16 [6144, 2048], P(('grp', 'ep'))
Inputs may be any that keep to these rules, and one draw needn't show every extreme that they name: `expert_ids`: each row names 8 different experts. In the rows of one device one expert, the same on all devices, is named by exactly 3 rows, and every other expert by at most 2 rows; some expert other than it is named by exactly 2 rows of a device. `slot_expert`: every expert is held by one or two slots; the expert named by 3 rows of every device is held by two. `cache_len`: some request has exactly 48 cached tokens. `gate_up`: slots holding the same expert hold equal weights. `down_proj`: slots holding the same expert hold equal weights.
All inputs are finite; a program needn't handle non-finite values.
Results may differ from a plain program's by a relative error of at most 0.033.
Values may be sent and summed in bfloat16 or wider, within the bound.
A program may use at most 128 MiB of HBM per device.

v0:
```python
import math
import jax
import jax.numpy as jnp
from jax import lax
from jax.sharding import PartitionSpec as P

D = 2048
HEADS = 32
KV_HEADS = 4
HEAD_DIM = 128
FF = 768
TOPK = 8
EXP_DEV = 2
SLOTS_DEV = 3
PRE = 8
masked_score = -1e30
epsilon = 1e-06


def prefill_context(queries, new_keys, new_values):
    head_group = HEADS // KV_HEADS
    scaling = 1.0 / math.sqrt(HEAD_DIM)
    query_pre = queries[:PRE].reshape(PRE, KV_HEADS, head_group, HEAD_DIM)
    keys_pre = new_keys[:PRE].reshape(PRE, KV_HEADS, HEAD_DIM)
    values_pre = new_values[:PRE].reshape(PRE, KV_HEADS, HEAD_DIM)
    scores = (
        jnp.einsum("ikgd,jkd->kgij", query_pre, keys_pre, preferred_element_type=jnp.float32)
        * scaling
    )
    causal = jnp.arange(PRE)[:, None] >= jnp.arange(PRE)[None, :]
    scores = jnp.where(causal, scores, masked_score)
    exponent = jnp.exp(scores - jnp.max(scores, axis=-1, keepdims=True))
    attn_probs = (exponent / jnp.sum(exponent, axis=-1, keepdims=True)).astype(jnp.bfloat16)
    mixed_values = jnp.einsum(
        "kgij,jkd->ikgd", attn_probs, values_pre, preferred_element_type=jnp.float32
    )
    return mixed_values.astype(jnp.bfloat16).reshape(PRE, HEADS * HEAD_DIM)


def decode_context(queries, new_keys, new_values, key_cache, value_cache, cache_len):
    requests = key_cache.shape[0]
    cache_slots = key_cache.shape[1]
    head_group = HEADS // KV_HEADS
    scaling = 1.0 / math.sqrt(HEAD_DIM)
    query_dec = queries[PRE:].reshape(requests, KV_HEADS, head_group, HEAD_DIM)
    keys_dec = new_keys[PRE:].reshape(requests, KV_HEADS, HEAD_DIM)
    values_dec = new_values[PRE:].reshape(requests, KV_HEADS, HEAD_DIM)
    cached_keys = key_cache.reshape(requests, cache_slots, KV_HEADS, HEAD_DIM)
    cached_values = value_cache.reshape(requests, cache_slots, KV_HEADS, HEAD_DIM)
    cache_scores = (
        jnp.einsum("nkgd,ntkd->nkgt", query_dec, cached_keys, preferred_element_type=jnp.float32)
        * scaling
    )
    own_score = (
        jnp.einsum("nkgd,nkd->nkg", query_dec, keys_dec, preferred_element_type=jnp.float32)
        * scaling
    )
    valid = jnp.arange(cache_slots)[None, :] < cache_len[:, None]
    cache_scores = jnp.where(valid[:, None, None, :], cache_scores, masked_score)
    top_score = jnp.maximum(jnp.max(cache_scores, axis=-1), own_score)
    cache_exp = jnp.exp(cache_scores - top_score[..., None])
    own_exp = jnp.exp(own_score - top_score)
    denominator = jnp.sum(cache_exp, axis=-1) + own_exp
    cache_probs = (cache_exp / denominator[..., None]).astype(jnp.bfloat16)
    own_probs = (own_exp / denominator).astype(jnp.bfloat16)
    mixed_values = jnp.einsum(
        "nkgt,ntkd->nkgd", cache_probs, cached_values, preferred_element_type=jnp.float32
    )
    mixed_values = (
        mixed_values
        + own_probs.astype(jnp.float32)[..., None] * values_dec.astype(jnp.float32)[:, :, None, :]
    )
    return mixed_values.astype(jnp.bfloat16).reshape(requests, HEADS * HEAD_DIM)


def activate(summed):
    return (jax.nn.silu(summed[..., :FF]) * summed[..., FF:]).astype(jnp.bfloat16)


def local(
    queries,
    new_keys,
    new_values,
    key_cache,
    value_cache,
    cache_len,
    residual,
    out_proj,
    norm_gain,
    expert_ids,
    route_weights,
    slot_expert,
    gate_up,
    down_proj,
):
    rows_dev = queries.shape[0]
    width_part = out_proj.shape[1]
    ep_devices = lax.axis_size("ep")
    group_devices = lax.axis_size("grp")
    experts_all = EXP_DEV * ep_devices
    most_rows = min(rows_dev, (TOPK * rows_dev + experts_all - 2) // (experts_all - 1) + 1)
    context = jnp.concatenate(
        [
            prefill_context(queries, new_keys, new_values),
            decode_context(queries, new_keys, new_values, key_cache, value_cache, cache_len),
        ],
        axis=0,
    )
    context_col, ids_col, weights_col = (
        lax.all_gather(context, "grp", axis=0, tiled=True),
        lax.all_gather(expert_ids, "grp", axis=0, tiled=True),
        lax.all_gather(route_weights, "grp", axis=0, tiled=True),
    )
    residual_col = lax.all_to_all(residual, "grp", split_axis=1, concat_axis=0, tiled=True)
    attended = (
        residual_col.astype(jnp.float32)
        + jnp.dot(context_col, out_proj, preferred_element_type=jnp.float32)
    ).astype(jnp.bfloat16)
    attended_f = attended.astype(jnp.float32)
    sum_squares = lax.psum(jnp.sum(attended_f * attended_f, axis=1), "grp")
    normed = (
        attended_f * lax.rsqrt(sum_squares / D + epsilon)[:, None] * norm_gain[None, :]
    ).astype(jnp.bfloat16)
    route_share = weights_col.astype(jnp.float32)
    route_share = route_share / jnp.sum(route_share, axis=-1, keepdims=True)
    column_rows = normed.shape[0]
    slot_rows = 2 * group_devices
    ep_index = lax.axis_index("ep")
    ids_all = lax.all_gather(ids_col, "ep", axis=0)
    share_all = lax.all_gather(route_share, "ep", axis=0)
    rows_all = lax.all_gather(normed, "ep", axis=0)
    mine = lax.dynamic_slice_in_dim(slot_expert, ep_index * SLOTS_DEV, SLOTS_DEV)
    slots = jnp.arange(slot_expert.shape[0], dtype=jnp.int32)
    same = slot_expert[None, :] == mine[:, None]
    copies = jnp.sum(same, axis=1)
    place = ep_index * SLOTS_DEV + jnp.arange(SLOTS_DEV)
    copy_index = jnp.sum(same & (slots[None, :] < place[:, None]), axis=1)
    hit = ids_all[:, None, :, :] == mine[None, :, None, None]
    share = jnp.sum(jnp.where(hit, share_all[:, None, :, :], 0.0), axis=-1)
    named = jnp.any(hit, axis=-1)
    count = named.astype(jnp.int32)
    ranking = jnp.cumsum(count, axis=-1) - count
    position = ranking // copies[None, :, None]
    taken = named & (ranking % copies[None, :, None] == copy_index[None, :, None])
    pick = taken[:, :, None, :] & (
        position[:, :, None, :] == jnp.arange(slot_rows)[None, None, :, None]
    )
    received = jnp.einsum(
        "sjtr,srd->jstd", pick.astype(jnp.bfloat16), rows_all, preferred_element_type=jnp.float32
    ).astype(jnp.bfloat16)
    received = received.reshape(SLOTS_DEV, ep_devices * slot_rows, width_part)
    partial_term = jnp.einsum(
        "jnd,jdf->jnf", received, gate_up, preferred_element_type=jnp.float32
    ).astype(jnp.bfloat16)
    summed = lax.psum_scatter(partial_term, "grp", scatter_dimension=1, tiled=True)
    hidden = activate(summed.astype(jnp.float32))
    hidden = lax.all_gather(hidden, "grp", axis=1, tiled=True)
    expert_out = jnp.einsum(
        "jnh,jhd->jnd", hidden, down_proj, preferred_element_type=jnp.float32
    ).astype(jnp.bfloat16)
    expert_out = expert_out.reshape(SLOTS_DEV, ep_devices, slot_rows, width_part)
    weighted = jnp.where(pick, share[:, :, None, :], 0.0).astype(jnp.bfloat16)
    mixture = jnp.einsum(
        "sjtr,jstd->srd", weighted, expert_out, preferred_element_type=jnp.float32
    ).astype(jnp.bfloat16)
    mixture = lax.psum_scatter(mixture, "ep", scatter_dimension=0, tiled=False)
    mixture = mixture.astype(jnp.float32)
    moe_col = mixture.astype(jnp.bfloat16)
    layer_col = (attended_f + mixture).astype(jnp.bfloat16)
    moe_out, layer_out = (
        lax.all_to_all(moe_col, "grp", split_axis=0, concat_axis=1, tiled=True),
        lax.all_to_all(layer_col, "grp", split_axis=0, concat_axis=1, tiled=True),
    )
    return (moe_out, layer_out)


def solution(mesh):
    placed = (
        P(("grp", "ep"), None),
        P(("grp", "ep"), None),
        P(("grp", "ep"), None),
        P(("grp", "ep"), None, None),
        P(("grp", "ep"), None, None),
        P(("grp", "ep")),
        P(("grp", "ep"), None),
        P(None, "grp"),
        P("grp"),
        P(("grp", "ep"), None),
        P(("grp", "ep"), None),
        P(),
        P("ep", "grp", None),
        P("ep", None, "grp"),
    )
    return jax.shard_map(
        local,
        mesh=mesh,
        in_specs=placed,
        out_specs=(P(("grp", "ep"), None), P(("grp", "ep"), None)),
        check_vma=False,
    )
```

profile of v0, /device:TPU:2, one launch (start us, length us, event | category | flops | bytes accessed | tf_op | source)
XLA Modules:
  0.0 433.6 jit_solution(6127606662466355972)
XLA Ops:
  7.2 1.7 copy.121
  8.9 6.1 %all-to-all-start = ((bf16[24,4,512]{2,0,1:T(8,128)(2,1)}), bf16[24,4,512]{2,0,1:T(8,128)(2,1)}, u32[]{:S(2)}, u32[]{:S(2)}) async-start(bf16[24,4,512]{2,0,1:T(8,128)(2,1)} %bitcast.118), calls=%async_computation | async-start | bytes 196608 | tf_op jit(solution)/shard_map/all_to_all | solution.py:114
  17.4 1.3 iota_compare_fusion.1
  22.6 1.3 fusion.55
  24.8 13.3 %all_gather.36 = bf16[96,4096]{1,0:T(8,128)(2,1)S(1)} all-gather(bf16[24,4096]{1,0:T(8,128)(2,1)S(1)} %pad_maximum_fusion), channel_id=1, replica_groups=mesh['grp'=4,'ep'=64] {'grp'}, dimensions={0}, use_global_device_ids=true | all-gather | bytes 983040 | tf_op jit(solution)/shard_map/all_gather | solution.py:110
  39.0 3.1 multiply_reduce_fusion
  42.1 9.6 %psum.7 = f32[96]{0:T(128)S(1)} all-reduce(f32[96]{0:T(128)S(1)} %get-tuple-element.12), channel_id=1, replica_groups=mesh['grp'=4,'ep'=64] {'grp'}, use_global_device_ids=true, to_apply=%region_11.12 | all-reduce | flops 96 | bytes 768 | tf_op jit(solution)/shard_map/psum | solution.py:120
  52.6 10.7 %all-gather.3 = s32[4,24,8]{1,2,0:T(8,128)S(1)} all-gather(s32[1,24,8]{1,2,0:T(8,128)S(1)} %bitcast.133), channel_id=1, replica_groups=mesh['grp'=4,'ep'=64] {'grp'}, dimensions={0}, use_global_device_ids=true | all-gather | bytes 3840 | tf_op jit(solution)/shard_map/all_gather | solution.py:111
  63.5 46.5 %all-gather.4 = s32[64,96,8]{1,2,0:T(8,128)S(1)} all-gather(s32[1,96,8]{1,2,0:T(8,128)S(1)} %reshape.156), channel_id=2, replica_groups=mesh['grp'=4,'ep'=64] {'ep'}, dimensions={0}, use_global_device_ids=true | all-gather | bytes 199680 | tf_op jit(solution)/shard_map/all_gather | solution.py:129
  113.7 21.2 %all-gather.12.cloned.1.call-done = bf16[6144,512]{1,0:T(8,128)(2,1)} async-done(((bf16[96,512]{1,0:T(8,128)(2,1)}), bf16[6144,512]{1,0:T(8,128)(2,1)}) %all-gather.12.cloned.1.call-update) | async-done | bytes 6291472 | tf_op jit(solution)/shard_map/all_gather | solution.py:131
  134.9 3.7 fusion.5
  138.6 6.6 %convolution_convert_fusion = bf16[3,512,1536]{2,1,0:T(8,128)(2,1)} fusion(bf16[3,512,1536]{2,1,0:T(8,128)(2,1)} %param.26, bf16[3,64,8,512]{3,2,0,1:T(8,128)(2,1)S(1)} %fusion.5), kind=kOutput, calls=%fused_computation.2 | convolution fusion | flops 2418278400 | bytes 11010048 | tf_op jit(solution)/shard_map/jnd,jdf->jnf/dot_general | solution.py:152
  145.3 49.2 %reduce-scatter.3.cloned.1.call-done = bf16[3,128,1536]{2,1,0:T(8,128)(2,1)} async-done(((bf16[3,512,1536]{2,1,0:T(8,128)(2,1)}), bf16[3,128,1536]{2,1,0:T(8,128)(2,1)}) %reduce-scatter.3.cloned.1.call-update) | async-done | bytes 1179664 | tf_op jit(solution)/shard_map/reduce_scatter | solution.py:155
  194.5 1.5 convert_element_type.126
  197.3 10.2 %all-gather.5 = bf16[4,24,8]{1,2,0:T(8,128)(2,1)S(1)} all-gather(bf16[1,24,8]{1,2,0:T(8,128)(2,1)S(1)} %bitcast.134), channel_id=1, replica_groups=mesh['grp'=4,'ep'=64] {'grp'}, dimensions={0}, use_global_device_ids=true | all-gather | bytes 1920 | tf_op jit(solution)/shard_map/all_gather | solution.py:112
  207.7 45.3 %all-gather.6 = f32[64,96,8]{1,2,0:T(8,128)S(1)} all-gather(f32[1,96,8]{1,2,0:T(8,128)S(1)} %divide_bitcast_fusion), channel_id=3, replica_groups=mesh['grp'=4,'ep'=64] {'ep'}, dimensions={0}, use_global_device_ids=true | all-gather | bytes 199680 | tf_op jit(solution)/shard_map/all_gather | solution.py:130
  253.4 3.0 fusion.4
  256.5 4.5 %bitcast_convert_fusion = bf16[64,96,512]{2,1,0:T(8,128)(2,1)} fusion(bf16[3,64,8,512]{3,2,1,0:T(8,128)(2,1)S(1)} %fusion.4, bf16[64,3,96]{2,1,0:T(4,128)(2,1)S(1)} %fusion.15, s32[64,3,96]{2,1,0:T(4,128)S(1)} %copy.59, pred[64,3,96]{2,1,0:T(4,128)(4,1)S(1)} %copy.58), kind=kOutput, calls=%fused_computation.1 | convolution fusion | flops 154583040 | bytes 7993344 | tf_op jit(solution)/shard_map/sjtr,jstd->srd/dot_general | solution.py:163
  261.0 147.2 %reduce-scatter.5.cloned.1.call-done = bf16[1,96,512]{2,1,0:T(8,128)(2,1)} async-done(((bf16[64,96,512]{2,1,0:T(8,128)(2,1)}), bf16[1,96,512]{2,1,0:T(8,128)(2,1)}) %reduce-scatter.5.cloned.1.call-update) | async-done | bytes 98320 | tf_op jit(solution)/shard_map/reduce_scatter | solution.py:166
  408.1 4.8 %all-to-all-start.1 = ((bf16[4,24,512]{2,1,0:T(8,128)(2,1)}), bf16[4,24,512]{2,1,0:T(8,128)(2,1)S(1)}, u32[]{:S(2)}, u32[]{:S(2)}) async-start(bf16[4,24,512]{2,1,0:T(8,128)(2,1)} %bitcast.125), calls=%async_computation.3 | async-start | bytes 196608 | tf_op jit(solution)/shard_map/all_to_all | solution.py:171
  413.0 1.6 fusion.29
  414.6 2.8 all-to-all-done.1
  417.3 4.7 %all-to-all-start.2 = ((bf16[4,24,512]{2,1,0:T(8,128)(2,1)}), bf16[4,24,512]{2,1,0:T(8,128)(2,1)S(1)}, u32[]{:S(2)}, u32[]{:S(2)}) async-start(bf16[4,24,512]{2,1,0:T(8,128)(2,1)} %bitcast.27), calls=%async_computation.4 | async-start | bytes 196608 | tf_op jit(solution)/shard_map/all_to_all | solution.py:172
  422.7 3.7 all-to-all-done.2
  (69 shorter events, 15.8 us)
Async XLA Ops:
  7.2 246.2 %copy-start = (bf16[3,768,512]{2,1,0:T(8,128)(2,1)S(1)}, bf16[3,768,512]{2,1,0:T(8,128)(2,1)}, u32[]{:S(2)}) copy-start(bf16[3,768,512]{2,1,0:T(8,128)(2,1)} %param.27) | copy-start | bytes 7077892
  7.2 15.4 %copy-start.1 = (bf16[16,48,512]{2,1,0:T(8,128)(2,1)S(1)}, bf16[16,48,512]{2,1,0:T(8,128)(2,1)}, u32[]{:S(2)}) copy-start(bf16[16,48,512]{2,1,0:T(8,128)(2,1)} %param.17) | copy-start | bytes 2359300
  8.9 29.2 %all-to-all-start = ((bf16[24,4,512]{2,0,1:T(8,128)(2,1)}), bf16[24,4,512]{2,0,1:T(8,128)(2,1)}, u32[]{:S(2)}, u32[]{:S(2)}) async-start(bf16[24,4,512]{2,0,1:T(8,128)(2,1)} %bitcast.118), calls=%async_computation | async-start | bytes 196608 | tf_op jit(solution)/shard_map/all_to_all | solution.py:114
  15.0 119.9 %all-gather.12.cloned.1.call-start = ((), (), s32[]{:S(2)}) async-start(), calls=%async_computation.8 | async-start | bytes 6389760 | tf_op jit(solution)/shard_map/all_gather | solution.py:131
  21.5 2.8 copy-start.6
  39.0 12.8 %copy-start.3 = (f32[512]{0:T(512)S(1)}, f32[512]{0:T(512)}, u32[]{:S(2)}) copy-start(f32[512]{0:T(512)} %param.22) | copy-start | bytes 6148
  39.0 13.6 %copy-start.2 = (s32[24,8]{0,1:T(8,128)S(1)}, s32[24,8]{0,1:T(8,128)}, u32[]{:S(2)}) copy-start(s32[24,8]{0,1:T(8,128)} %param.23) | copy-start | bytes 2308
  39.0 24.4 %copy-start.5 = (s32[192]{0:T(256)S(1)}, s32[192]{0:T(256)}, u32[]{:S(2)}) copy-start(s32[192]{0:T(256)} %param.25) | copy-start | bytes 2308
  52.5 142.0 %reduce-scatter.3.cloned.1.call-start = ((), (), s32[]{:S(2)}) async-start(), calls=%async_computation.5 | async-start | bytes 5898240 | tf_op jit(solution)/shard_map/reduce_scatter | solution.py:155
  145.3 108.1 %all-gather.10.cloned.1.call-start = ((), (), s32[]{:S(2)}) async-start(), calls=%async_computation.6 | async-start | bytes 2949120 | tf_op jit(solution)/shard_map/all_gather | solution.py:157
  196.0 1.3 copy-start.4
  197.3 210.9 %reduce-scatter.5.cloned.1.call-start = ((), (), s32[]{:S(2)}) async-start(), calls=%async_computation.7 | async-start | bytes 6389760 | tf_op jit(solution)/shard_map/reduce_scatter | solution.py:166
  408.1 9.2 %all-to-all-start.1 = ((bf16[4,24,512]{2,1,0:T(8,128)(2,1)}), bf16[4,24,512]{2,1,0:T(8,128)(2,1)S(1)}, u32[]{:S(2)}, u32[]{:S(2)}) async-start(bf16[4,24,512]{2,1,0:T(8,128)(2,1)} %bitcast.125), calls=%async_computation.3 | async-start | bytes 196608 | tf_op jit(solution)/shard_map/all_to_all | solution.py:171
  417.3 9.1 %all-to-all-start.2 = ((bf16[4,24,512]{2,1,0:T(8,128)(2,1)}), bf16[4,24,512]{2,1,0:T(8,128)(2,1)S(1)}, u32[]{:S(2)}, u32[]{:S(2)}) async-start(bf16[4,24,512]{2,1,0:T(8,128)(2,1)} %bitcast.27), calls=%async_computation.4 | async-start | bytes 196608 | tf_op jit(solution)/shard_map/all_to_all | solution.py:172
Sparse Core Ops, SparseCore 0:
  52.6 82.2 all-gather.11
  145.4 49.0 reduce-scatter.2
  197.4 35.6 all-gather.9
  261.1 147.0 reduce-scatter.4
where the time goes:
time: 435 us; the launch traced here: 434 us
  waiting for transfers between devices  224 us (51%)
  blocking collectives  136 us (31%)
  matrix products  24.9 us (6%)
  starting transfers between devices  15.8 us (4%)
  between operations  14 us (3%)
  other arithmetic  12.9 us (3%)
  local copies, waits for them, and re-layouts  6.18 us (1%)
    reduce_scatter x1, waiting for transfers between devices, local(): mixture = lax.psum_scatter(mixture, 'ep', scatter_dimension=0, tiled=False)  147 us
    reduce_scatter x1, waiting for transfers between devices, local(): lax.psum_scatter(partial_term, 'grp', scatter_dimension=1, tiled=True)  49.2 us
    all_gather x1, blocking collectives, local(): ids_all = lax.all_gather(ids_col, 'ep', axis=0)  46.5 us
    all_gather x1, blocking collectives, local(): share_all = lax.all_gather(route_share, 'ep', axis=0)  45.3 us
    all_gather x1, waiting for transfers between devices, local(): rows_all = lax.all_gather(normed, 'ep', axis=0)  21.2 us
    all_gather x1, blocking collectives, local(): lax.all_gather(context, 'grp', axis=0, tiled=True)  13.3 us
    all_gather x1, blocking collectives, local(): lax.all_gather(expert_ids, 'grp', axis=0, tiled=True)  10.7 us
    all_gather x1, blocking collectives, local(): lax.all_gather(route_weights, 'grp', axis=0, tiled=True)  10.2 us
  transfers between devices with their start and end apart: 7, of which 5 were waited for; matrix products, arithmetic and copies ran while one was open for 4% of the time, Pallas kernels for 0%

commit v1 on v0

--- a/solution.py
+++ b/solution.py
@@ -108,7 +108,12 @@
     )
     context_col, ids_col, weights_col = (
         lax.all_gather(context, "grp", axis=0, tiled=True),
-        lax.all_gather(expert_ids, "grp", axis=0, tiled=True),
+        jnp.concatenate(
+            jax.lax.all_to_all(
+                jnp.stack(jax.lax.axis_size("grp") * [expert_ids], axis=0), "grp", 0, 0
+            ),
+            0,
+        ),
         lax.all_gather(route_weights, "grp", axis=0, tiled=True),
     )
     residual_col = lax.all_to_all(residual, "grp", split_axis=1, concat_axis=0, tiled=True)

time: 435 us -> 434 us (level)
  blocking collectives: 136 us -> 126 us
  starting transfers between devices: 15.8 us -> 20.3 us
    all_gather x1 -> x0, blocking collectives: 10.7 us -> none  [local(): lax.all_gather(expert_ids, 'grp', axis=0, tiled=True)]
    all_to_all x0 -> x1, starting transfers between devices: none -> 4.56 us  [local(): jax.lax.all_to_all(jnp.stack(jax.lax.axis_size('grp') * [expert_ids], axi...]
  transfers between devices with their start and end apart: 7 -> 8, of which waited for: 5 -> 6; matrix products, arithmetic and copies ran while one was open for 4% -> 4% of each run, Pallas kernels for 0% -> 0%
where the time goes in v1:
time: 434 us; the launch traced here: 433 us
  waiting for transfers between devices  227 us (52%)
  blocking collectives  126 us (29%)
  matrix products  24.9 us (6%)
  starting transfers between devices  20.3 us (5%)
  between operations  14 us (3%)
  other arithmetic  13.6 us (3%)
  local copies, waits for them, and re-layouts  7.44 us (2%)
    reduce_scatter x1, waiting for transfers between devices, local(): mixture = lax.psum_scatter(mixture, 'ep', scatter_dimension=0, tiled=False)  147 us
    reduce_scatter x1, waiting for transfers between devices, local(): lax.psum_scatter(partial_term, 'grp', scatter_dimension=1, tiled=True)  49.2 us
    all_gather x1, blocking collectives, local(): ids_all = lax.all_gather(ids_col, 'ep', axis=0)  47.2 us
    all_gather x1, blocking collectives, local(): share_all = lax.all_gather(route_share, 'ep', axis=0)  45.2 us
    all_gather x1, waiting for transfers between devices, local(): rows_all = lax.all_gather(normed, 'ep', axis=0)  21.3 us
    all_gather x1, blocking collectives, local(): lax.all_gather(context, 'grp', axis=0, tiled=True)  13.3 us
    all_gather x1, blocking collectives, local(): lax.all_gather(route_weights, 'grp', axis=0, tiled=True)  10.2 us
    psum x1, blocking collectives, local(): sum_squares = lax.psum(jnp.sum(attended_f * attended_f, axis=1), 'grp')  9.61 us
  transfers between devices with their start and end apart: 8, of which 6 were waited for; matrix products, arithmetic and copies ran while one was open for 4% of the time, Pallas kernels for 0%

profile of v1, /device:TPU:2, one launch (start us, length us, event | category | flops | bytes accessed | tf_op | source)
XLA Modules:
  0.0 433.2 jit_solution(17004051154045625159)
XLA Ops:
  7.2 1.7 copy.135
  8.9 6.1 %all-to-all-start.1 = ((bf16[24,4,512]{2,0,1:T(8,128)(2,1)}), bf16[24,4,512]{2,0,1:T(8,128)(2,1)}, u32[]{:S(2)}, u32[]{:S(2)}) async-start(bf16[24,4,512]{2,0,1:T(8,128)(2,1)} %bitcast.120), calls=%async_computation.1 | async-start | bytes 196608 | tf_op jit(solution)/shard_map/all_to_all | solution.py:119
  17.4 1.3 iota_compare_fusion.1
  24.8 13.3 %all_gather.28 = bf16[96,4096]{1,0:T(8,128)(2,1)S(1)} all-gather(bf16[24,4096]{1,0:T(8,128)(2,1)S(1)} %pad_maximum_fusion), channel_id=1, replica_groups=mesh['grp'=4,'ep'=64] {'grp'}, dimensions={0}, use_global_device_ids=true | all-gather | bytes 983040 | tf_op jit(solution)/shard_map/all_gather | solution.py:110
  39.0 3.1 multiply_reduce_fusion
  42.1 9.6 %psum.7 = f32[96]{0:T(128)S(1)} all-reduce(f32[96]{0:T(128)S(1)} %get-tuple-element.12), channel_id=1, replica_groups=mesh['grp'=4,'ep'=64] {'grp'}, use_global_device_ids=true, to_apply=%region_11.12 | all-reduce | flops 96 | bytes 768 | tf_op jit(solution)/shard_map/psum | solution.py:125
  53.2 4.6 %all-to-all-start = ((s32[4,1,192]{2,1,0:T(1,128)}), s32[4,1,192]{2,1,0:T(1,128)S(1)}, u32[]{:S(2)}, u32[]{:S(2)}) async-start(s32[4,1,192]{2,1,0:T(1,128)} %reshape.170), calls=%async_computation | async-start | bytes 8192 | tf_op jit(solution)/shard_map/all_to_all | solution.py:112
  58.1 3.5 all-to-all-done
  63.0 47.2 %all_gather.24 = s32[64,96,8]{1,2,0:T(8,128)S(1)} all-gather(s32[1,96,8]{1,2,0:T(8,128)S(1)} %all_gather_reshape.3), channel_id=1, replica_groups=mesh['grp'=4,'ep'=64] {'ep'}, dimensions={0}, use_global_device_ids=true | all-gather | bytes 199680 | tf_op jit(solution)/shard_map/all_gather | solution.py:134
  113.6 21.3 %all-gather.9.cloned.1.call-done = bf16[6144,512]{1,0:T(8,128)(2,1)} async-done(((bf16[96,512]{1,0:T(8,128)(2,1)}), bf16[6144,512]{1,0:T(8,128)(2,1)}) %all-gather.9.cloned.1.call-update) | async-done | bytes 6291472 | tf_op jit(solution)/shard_map/all_gather | solution.py:136
  134.9 3.7 fusion.5
  138.6 6.6 %convolution_convert_fusion = bf16[3,512,1536]{2,1,0:T(8,128)(2,1)} fusion(bf16[3,512,1536]{2,1,0:T(8,128)(2,1)} %param.26, bf16[3,64,8,512]{3,2,0,1:T(8,128)(2,1)S(1)} %fusion.5), kind=kOutput, calls=%fused_computation.2 | convolution fusion | flops 2418278400 | bytes 11010048 | tf_op jit(solution)/shard_map/jnd,jdf->jnf/dot_general | solution.py:157
  145.3 49.2 %reduce-scatter.3.cloned.1.call-done = bf16[3,128,1536]{2,1,0:T(8,128)(2,1)} async-done(((bf16[3,512,1536]{2,1,0:T(8,128)(2,1)}), bf16[3,128,1536]{2,1,0:T(8,128)(2,1)}) %reduce-scatter.3.cloned.1.call-update) | async-done | bytes 1179664 | tf_op jit(solution)/shard_map/reduce_scatter | solution.py:160
  194.5 1.5 convert_element_type.126
  197.3 10.2 %all-gather.2 = bf16[4,24,8]{1,2,0:T(8,128)(2,1)S(1)} all-gather(bf16[1,24,8]{1,2,0:T(8,128)(2,1)S(1)} %bitcast.136), channel_id=1, replica_groups=mesh['grp'=4,'ep'=64] {'grp'}, dimensions={0}, use_global_device_ids=true | all-gather | bytes 1920 | tf_op jit(solution)/shard_map/all_gather | solution.py:117
  207.7 45.2 %all-gather.3 = f32[64,96,8]{1,2,0:T(8,128)S(1)} all-gather(f32[1,96,8]{1,2,0:T(8,128)S(1)} %divide_bitcast_fusion), channel_id=2, replica_groups=mesh['grp'=4,'ep'=64] {'ep'}, dimensions={0}, use_global_device_ids=true | all-gather | bytes 199680 | tf_op jit(solution)/shard_map/all_gather | solution.py:135
  253.4 3.0 fusion.4
  256.5 4.5 %bitcast_convert_fusion = bf16[64,96,512]{2,1,0:T(8,128)(2,1)} fusion(bf16[3,64,8,512]{3,2,1,0:T(8,128)(2,1)S(1)} %fusion.4, bf16[64,3,96]{2,1,0:T(4,128)(2,1)S(1)} %fusion.15, s32[64,3,96]{2,1,0:T(4,128)S(1)} %copy.73, pred[64,3,96]{2,1,0:T(4,128)(4,1)S(1)} %copy.72), kind=kOutput, calls=%fused_computation.1 | convolution fusion | flops 154583040 | bytes 7993344 | tf_op jit(solution)/shard_map/sjtr,jstd->srd/dot_general | solution.py:168
  261.0 146.9 %reduce-scatter.5.cloned.1.call-done = bf16[1,96,512]{2,1,0:T(8,128)(2,1)} async-done(((bf16[64,96,512]{2,1,0:T(8,128)(2,1)}), bf16[1,96,512]{2,1,0:T(8,128)(2,1)}) %reduce-scatter.5.cloned.1.call-update) | async-done | bytes 98320 | tf_op jit(solution)/shard_map/reduce_scatter | solution.py:171
  407.9 4.7 %all-to-all-start.2 = ((bf16[4,24,512]{2,1,0:T(8,128)(2,1)}), bf16[4,24,512]{2,1,0:T(8,128)(2,1)S(1)}, u32[]{:S(2)}, u32[]{:S(2)}) async-start(bf16[4,24,512]{2,1,0:T(8,128)(2,1)} %bitcast.127), calls=%async_computation.4 | async-start | bytes 196608 | tf_op jit(solution)/shard_map/all_to_all | solution.py:176
  412.6 1.6 fusion.29
  414.2 2.8 all-to-all-done.2
  416.9 4.7 %all-to-all-start.3 = ((bf16[4,24,512]{2,1,0:T(8,128)(2,1)}), bf16[4,24,512]{2,1,0:T(8,128)(2,1)S(1)}, u32[]{:S(2)}, u32[]{:S(2)}) async-start(bf16[4,24,512]{2,1,0:T(8,128)(2,1)} %bitcast.26), calls=%async_computation.5 | async-start | bytes 196608 | tf_op jit(solution)/shard_map/all_to_all | solution.py:177
  422.3 3.7 all-to-all-done.3
  (75 shorter events, 19.0 us)
Async XLA Ops:
  7.2 246.2 %copy-start = (bf16[3,768,512]{2,1,0:T(8,128)(2,1)S(1)}, bf16[3,768,512]{2,1,0:T(8,128)(2,1)}, u32[]{:S(2)}) copy-start(bf16[3,768,512]{2,1,0:T(8,128)(2,1)} %param.27) | copy-start | bytes 7077892
  7.2 15.4 %copy-start.1 = (bf16[16,48,512]{2,1,0:T(8,128)(2,1)S(1)}, bf16[16,48,512]{2,1,0:T(8,128)(2,1)}, u32[]{:S(2)}) copy-start(bf16[16,48,512]{2,1,0:T(8,128)(2,1)} %param.17) | copy-start | bytes 2359300
  8.9 29.2 %all-to-all-start.1 = ((bf16[24,4,512]{2,0,1:T(8,128)(2,1)}), bf16[24,4,512]{2,0,1:T(8,128)(2,1)}, u32[]{:S(2)}, u32[]{:S(2)}) async-start(bf16[24,4,512]{2,0,1:T(8,128)(2,1)} %bitcast.120), calls=%async_computation.1 | async-start | bytes 196608 | tf_op jit(solution)/shard_map/all_to_all | solution.py:119
  15.0 119.9 %all-gather.9.cloned.1.call-start = ((), (), s32[]{:S(2)}) async-start(), calls=%async_computation.9 | async-start | bytes 6389760 | tf_op jit(solution)/shard_map/all_gather | solution.py:136
  21.5 2.8 copy-start.6
  39.0 12.8 %copy-start.3 = (f32[512]{0:T(512)S(1)}, f32[512]{0:T(512)}, u32[]{:S(2)}) copy-start(f32[512]{0:T(512)} %param.22) | copy-start | bytes 6148
  39.0 13.5 %copy-start.2 = (s32[24,8]{0,1:T(8,128)S(1)}, s32[24,8]{0,1:T(8,128)}, u32[]{:S(2)}) copy-start(s32[24,8]{0,1:T(8,128)} %param.23) | copy-start | bytes 2308
  39.0 18.8 %copy-start.5 = (s32[192]{0:T(256)S(1)}, s32[192]{0:T(256)}, u32[]{:S(2)}) copy-start(s32[192]{0:T(256)} %param.25) | copy-start | bytes 2308
  53.2 8.4 %all-to-all-start = ((s32[4,1,192]{2,1,0:T(1,128)}), s32[4,1,192]{2,1,0:T(1,128)S(1)}, u32[]{:S(2)}, u32[]{:S(2)}) async-start(s32[4,1,192]{2,1,0:T(1,128)} %reshape.170), calls=%async_computation | async-start | bytes 8192 | tf_op jit(solution)/shard_map/all_to_all | solution.py:112
  57.8 136.7 %reduce-scatter.3.cloned.1.call-start = ((), (), s32[]{:S(2)}) async-start(), calls=%async_computation.6 | async-start | bytes 5898240 | tf_op jit(solution)/shard_map/reduce_scatter | solution.py:160
  145.3 108.1 %all-gather.7.cloned.1.call-start = ((), (), s32[]{:S(2)}) async-start(), calls=%async_computation.7 | async-start | bytes 2949120 | tf_op jit(solution)/shard_map/all_gather | solution.py:162
  196.0 1.3 copy-start.4
  197.3 210.6 %reduce-scatter.5.cloned.1.call-start = ((), (), s32[]{:S(2)}) async-start(), calls=%async_computation.8 | async-start | bytes 6389760 | tf_op jit(solution)/shard_map/reduce_scatter | solution.py:171
  407.9 9.1 %all-to-all-start.2 = ((bf16[4,24,512]{2,1,0:T(8,128)(2,1)}), bf16[4,24,512]{2,1,0:T(8,128)(2,1)S(1)}, u32[]{:S(2)}, u32[]{:S(2)}) async-start(bf16[4,24,512]{2,1,0:T(8,128)(2,1)} %bitcast.127), calls=%async_computation.4 | async-start | bytes 196608 | tf_op jit(solution)/shard_map/all_to_all | solution.py:176
  416.9 9.1 %all-to-all-start.3 = ((bf16[4,24,512]{2,1,0:T(8,128)(2,1)}), bf16[4,24,512]{2,1,0:T(8,128)(2,1)S(1)}, u32[]{:S(2)}, u32[]{:S(2)}) async-start(bf16[4,24,512]{2,1,0:T(8,128)(2,1)} %bitcast.26), calls=%async_computation.5 | async-start | bytes 196608 | tf_op jit(solution)/shard_map/all_to_all | solution.py:177
Sparse Core Ops, SparseCore 0:
  52.6 82.2 all-gather.8
  145.4 49.0 reduce-scatter.2
  197.4 35.6 all-gather.6
  261.1 146.7 reduce-scatter.4
